TPU v7x, 32 devices: a whole 2x2x4 slice. The times are simulated.
32 devices in a mesh: seq: 16 (over z, x, core), wshard: 2 (over y).
Axes of the slice: x: 2, y: 2, z: 4, core: 2. Of those that a mesh axis runs over, the one named last changes fastest.
Arguments:
- inputs: bfloat16 [8192, 640], P(('seq', 'wshard')), may hold values from -6 to 6
- doc_ids: int32 [8192], P(('seq', 'wshard')), may hold values from 0 to 2, never falling along the last dimension, each value on 1 to 4096 neighbouring positions
- w_query: bfloat16 [640, 1024], P('wshard'), may hold values from -0.25 to 0.25
- w_key: bfloat16 [640, 256], P('wshard'), may hold values from -0.25 to 0.25
- w_value: bfloat16 [640, 256], P('wshard'), may hold values from -0.25 to 0.25
- w_out: bfloat16 [1024, 640], P('wshard'), may hold values from -0.1875 to 0.1875
- w_gate: bfloat16 [640, 2048], P('wshard'), may hold values from -0.25 to 0.25
- w_up: bfloat16 [640, 2048], P('wshard'), may hold values from -0.25 to 0.25
- w_down: bfloat16 [2048, 640], P('wshard'), may hold values from -0.125 to 0.125
- gain_in: bfloat16 [640], P('wshard'), may hold values from -0.5 to 1
- gain_attn_post: bfloat16 [640], P('wshard'), may hold values from -0.5 to 1
- gain_ff_pre: bfloat16 [640], P('wshard'), may hold values from -0.5 to 1
- gain_ff_post: bfloat16 [640], P('wshard'), may hold values from -0.5 to 1
- gain_query: bfloat16 [256], P('wshard'), may hold values from -0.5 to 1
- gain_key: bfloat16 [256], P('wshard'), may hold values from -0.5 to 1
- cotangent: bfloat16 [8192, 640], P(('seq', 'wshard')), may hold values from -6 to 6
Outputs:
- layer_out: bfloat16 [8192, 640], P(('seq', 'wshard'))
- grad_inputs: float32 [8192, 640], P(('seq', 'wshard'))
- grad_w_query: float32 [640, 1024], P('wshard')
- grad_w_key: float32 [640, 256], P('wshard')
- grad_w_value: float32 [640, 256], P('wshard')
- grad_w_out: float32 [1024, 640], P('wshard')
- grad_w_gate: float32 [640, 2048], P('wshard')
- grad_w_up: float32 [640, 2048], P('wshard')
- grad_w_down: float32 [2048, 640], P('wshard')
- grad_gain_in: float32 [640], P('wshard')
- grad_gain_attn_post: float32 [640], P('wshard')
- grad_gain_ff_pre: float32 [640], P('wshard')
- grad_gain_ff_post: float32 [640], P('wshard')
- grad_gain_query: float32 [256], P('wshard')
- grad_gain_key: float32 [256], P('wshard')
Inputs may be any that keep to these rules, and one draw needn't show every extreme that they name: `doc_ids`: document numbers never fall along the token stream; every document has 1 to 4096 tokens, one exactly 4096.
All inputs are finite; a program needn't handle non-finite values.
Results may differ from a plain program's by a relative error of at most 0.025.
Values may be sent and summed in bfloat16 or wider, within the bound.
A program may use at most 128 MiB of HBM per device.

v0:
```python
import jax
import jax.numpy as jnp
from jax import lax
from jax.sharding import PartitionSpec as P

WINDOW = 512
NORM_EPSILON = 1e-06
ROPE_BASE = 10000.0
MASK_FLOOR = -1e30


def from_behind(array, axis, by):
    count = lax.axis_size(axis)
    pairs = [(i, i + by) for i in range(count) if 0 <= i + by < count]
    return lax.ppermute(array, axis, pairs)


def rms_gain(tensor, gain_vec):
    factor = lax.rsqrt(jnp.mean(tensor * tensor, axis=-1, keepdims=True) + NORM_EPSILON)
    return tensor * factor * (1.0 + gain_vec)


def rope_tables(positions, head_width):
    half_width = head_width // 2
    exponent = jnp.arange(half_width, dtype=jnp.float32) * (2.0 / head_width)
    inverse = jnp.exp(-jnp.log(ROPE_BASE) * exponent)
    angles = positions.astype(jnp.float32)[:, None] * inverse[None, :]
    return (jnp.cos(angles), jnp.sin(angles))


def norm_rope(tensor, gain_vec, cos_table, sin_table):
    normed = rms_gain(tensor, gain_vec)
    half_width = tensor.shape[-1] // 2
    front_part = normed[..., :half_width]
    back_part = normed[..., half_width:]
    cos_rows = cos_table[:, None, :]
    sin_rows = sin_table[:, None, :]
    return jnp.concatenate(
        [
            front_part * cos_rows - back_part * sin_rows,
            back_part * cos_rows + front_part * sin_rows,
        ],
        axis=-1,
    )


def geglu(gate_pre, up_pre):
    return jax.nn.gelu(gate_pre, approximate=True) * up_pre


def window_mask(query_pos, key_pos, query_doc, key_doc):
    distance = query_pos[:, None] - key_pos[None, :]
    return (
        (distance >= 0)
        & (distance < WINDOW)
        & (key_pos[None, :] >= 0)
        & (query_doc[:, None] == key_doc[None, :])
    )


def masked_scores(queries, all_keys, allowed, score_scale):
    scores = (
        jnp.einsum("qhd,kd->hqk", queries, all_keys, preferred_element_type=jnp.float32)
        * score_scale
    )
    return jnp.where(allowed[None], scores, MASK_FLOOR)


def weight_grad(left_rows, right_rows):
    return jnp.einsum("tc,tf->cf", left_rows, right_rows, preferred_element_type=jnp.float32)


def per_device(
    inputs,
    doc_ids,
    w_query,
    w_key,
    w_value,
    w_out,
    w_gate,
    w_up,
    w_down,
    gain_in,
    gain_attn_post,
    gain_ff_pre,
    gain_ff_post,
    gain_query,
    gain_key,
    cotangent,
):
    gathered = (
        lax.all_gather(w_query, "wshard", axis=0, tiled=True),
        lax.all_gather(w_key, "wshard", axis=0, tiled=True),
        lax.all_gather(w_value, "wshard", axis=0, tiled=True),
        lax.all_gather(w_out, "wshard", axis=0, tiled=True),
        lax.all_gather(w_gate, "wshard", axis=0, tiled=True),
        lax.all_gather(w_up, "wshard", axis=0, tiled=True),
        lax.all_gather(w_down, "wshard", axis=0, tiled=True),
        lax.all_gather(gain_in, "wshard", axis=0, tiled=True),
        lax.all_gather(gain_attn_post, "wshard", axis=0, tiled=True),
        lax.all_gather(gain_ff_pre, "wshard", axis=0, tiled=True),
        lax.all_gather(gain_ff_post, "wshard", axis=0, tiled=True),
        lax.all_gather(gain_query, "wshard", axis=0, tiled=True),
        lax.all_gather(gain_key, "wshard", axis=0, tiled=True),
    )
    full_query, full_key, full_value, full_out, full_gate, full_up, full_down = gathered[:7]
    in_gain, attn_post_gain, ff_pre_gain, ff_post_gain, query_gain, key_gain = [
        g.astype(jnp.float32) for g in gathered[7:]
    ]
    row_count = inputs.shape[0]
    head_dim = full_key.shape[1]
    head_count = full_query.shape[1] // head_dim
    score_scale = head_dim ** (-0.5)
    start_row = lax.axis_index(("seq", "wshard")) * row_count
    query_pos = start_row + jnp.arange(row_count, dtype=jnp.int32)
    cos_table, sin_table = rope_tables(query_pos, head_dim)
    x_float = inputs.astype(jnp.float32)
    normed_in = rms_gain(x_float, in_gain).astype(jnp.bfloat16)
    query_raw = jnp.dot(normed_in, full_query, preferred_element_type=jnp.float32).reshape(
        row_count, head_count, head_dim
    )
    key_raw = jnp.dot(normed_in, full_key, preferred_element_type=jnp.float32)[:, None, :]
    values = jnp.dot(normed_in, full_value, preferred_element_type=jnp.float32).astype(jnp.bfloat16)
    queries = norm_rope(query_raw, query_gain, cos_table, sin_table).astype(jnp.bfloat16)
    key_rot = norm_rope(key_raw, key_gain, cos_table, sin_table)[:, 0].astype(jnp.bfloat16)
    sent_rows = min(WINDOW, row_count)
    hop_count = WINDOW // sent_rows
    outgoing = (key_rot, values, doc_ids)
    halo_keys = []
    halo_values = []
    halo_docs = []
    for distance in range(hop_count, 0, -1):
        arrived = from_behind((outgoing[0], outgoing[1], outgoing[2]), ("seq", "wshard"), distance)
        halo_keys.append(arrived[0])
        halo_values.append(arrived[1])
        halo_docs.append(arrived[2])
    all_keys = jnp.concatenate(halo_keys + [key_rot], 0)
    all_values = jnp.concatenate(halo_values + [values], 0)
    all_docs = jnp.concatenate(halo_docs + [doc_ids], 0)
    key_pos = start_row - WINDOW + jnp.arange(WINDOW + row_count, dtype=jnp.int32)
    allowed = window_mask(query_pos, key_pos, doc_ids, all_docs)
    scores = masked_scores(queries, all_keys, allowed, score_scale)
    row_peak = jnp.max(scores, axis=-1, keepdims=True)
    row_total = jnp.sum(
        jnp.where(allowed[None], jnp.exp(scores - row_peak), 0.0), axis=-1, keepdims=True
    )
    log_total = row_peak + jnp.log(row_total)
    soft = jnp.where(allowed[None], jnp.exp(scores - log_total), 0.0).astype(jnp.bfloat16)
    attended = jnp.einsum("hqk,kd->qhd", soft, all_values, preferred_element_type=jnp.float32)
    attended = attended.reshape(row_count, head_count * head_dim).astype(jnp.bfloat16)
    attn_proj = jnp.dot(attended, full_out, preferred_element_type=jnp.float32)
    resid = x_float + rms_gain(attn_proj, attn_post_gain)
    normed_ff = rms_gain(resid, ff_pre_gain).astype(jnp.bfloat16)
    gate_pre = jnp.dot(normed_ff, full_gate, preferred_element_type=jnp.float32)
    up_pre = jnp.dot(normed_ff, full_up, preferred_element_type=jnp.float32)
    hidden = geglu(gate_pre, up_pre).astype(jnp.bfloat16)
    ff_proj = jnp.dot(hidden, full_down, preferred_element_type=jnp.float32)
    layer_out = (resid + rms_gain(ff_proj, ff_post_gain)).astype(jnp.bfloat16)
    grad_top = cotangent.astype(jnp.float32)
    _, pullback = jax.vjp(rms_gain, ff_proj, ff_post_gain)
    grad_ff_proj, grad_gain_ff_post = pullback(grad_top)
    grad_ff_proj = grad_ff_proj.astype(jnp.bfloat16)
    grad_w_down = weight_grad(hidden, grad_ff_proj)
    grad_hidden = lax.dot_general(
        grad_ff_proj, full_down, (((1,), (1,)), ((), ())), preferred_element_type=jnp.float32
    )
    _, pullback = jax.vjp(geglu, gate_pre, up_pre)
    grad_gate, grad_up = pullback(grad_hidden)
    grad_gate = grad_gate.astype(jnp.bfloat16)
    grad_up = grad_up.astype(jnp.bfloat16)
    grad_w_gate = weight_grad(normed_ff, grad_gate)
    grad_w_up = weight_grad(normed_ff, grad_up)
    grad_normed_ff = lax.dot_general(
        grad_gate, full_gate, (((1,), (1,)), ((), ())), preferred_element_type=jnp.float32
    )
    grad_normed_ff = grad_normed_ff + lax.dot_general(
        grad_up, full_up, (((1,), (1,)), ((), ())), preferred_element_type=jnp.float32
    )
    _, pullback = jax.vjp(rms_gain, resid, ff_pre_gain)
    grad_resid_part, grad_gain_ff_pre = pullback(grad_normed_ff)
    grad_resid = grad_top + grad_resid_part
    ff_gradients = (grad_w_gate, grad_w_up, grad_w_down, grad_gain_ff_pre, grad_gain_ff_post)
    ff_parts = (
        lax.psum_scatter(
            ff_gradients[0].astype(jnp.bfloat16), "wshard", scatter_dimension=0, tiled=True
        ).astype(jnp.float32),
        lax.psum_scatter(
            ff_gradients[1].astype(jnp.bfloat16), "wshard", scatter_dimension=0, tiled=True
        ).astype(jnp.float32),
        lax.psum_scatter(
            ff_gradients[2].astype(jnp.bfloat16), "wshard", scatter_dimension=0, tiled=True
        ).astype(jnp.float32),
        lax.psum_scatter(
            ff_gradients[3].astype(jnp.bfloat16), "wshard", scatter_dimension=0, tiled=True
        ).astype(jnp.float32),
        lax.psum_scatter(
            ff_gradients[4].astype(jnp.bfloat16), "wshard", scatter_dimension=0, tiled=True
        ).astype(jnp.float32),
    )
    ff_reduced = (
        lax.psum(ff_parts[0].astype(jnp.bfloat16), "seq").astype(jnp.float32),
        lax.psum(ff_parts[1].astype(jnp.bfloat16), "seq").astype(jnp.float32),
        lax.psum(ff_parts[2].astype(jnp.bfloat16), "seq").astype(jnp.float32),
        lax.psum(ff_parts[3].astype(jnp.bfloat16), "seq").astype(jnp.float32),
        lax.psum(ff_parts[4].astype(jnp.bfloat16), "seq").astype(jnp.float32),
    )
    _, pullback = jax.vjp(rms_gain, attn_proj, attn_post_gain)
    grad_attn_proj, grad_gain_attn_post = pullback(grad_resid)
    grad_attn_proj = grad_attn_proj.astype(jnp.bfloat16)
    grad_w_out = weight_grad(attended, grad_attn_proj)
    grad_attended = lax.dot_general(
        grad_attn_proj, full_out, (((1,), (1,)), ((), ())), preferred_element_type=jnp.float32
    ).astype(jnp.bfloat16)
    grad_heads = grad_attended.reshape(row_count, head_count, head_dim)
    again_scores = masked_scores(queries, all_keys, allowed, score_scale)
    probs = jnp.where(allowed[None], jnp.exp(again_scores - log_total), 0.0)
    grad_soft = jnp.einsum(
        "qhd,kd->hqk", grad_heads, all_values, preferred_element_type=jnp.float32
    )
    row_inner = jnp.sum(probs * grad_soft, axis=-1, keepdims=True)
    grad_score = (probs * (grad_soft - row_inner) * score_scale).astype(jnp.bfloat16)
    grad_queries = jnp.einsum(
        "hqk,kd->qhd", grad_score, all_keys, preferred_element_type=jnp.float32
    )
    grad_keys_all = jnp.einsum(
        "hqk,qhd->kd", grad_score, queries, preferred_element_type=jnp.float32
    )
    grad_values_all = jnp.einsum(
        "hqk,qhd->kd", probs.astype(jnp.bfloat16), grad_heads, preferred_element_type=jnp.float32
    )
    back_keys = jnp.zeros((sent_rows, head_dim), jnp.float32)
    back_values = jnp.zeros((sent_rows, head_dim), jnp.float32)
    for piece_index in range(hop_count):
        distance = hop_count - piece_index
        piece_start = piece_index * sent_rows
        arrived = (
            from_behind(
                grad_keys_all[piece_start : piece_start + sent_rows].astype(jnp.bfloat16),
                ("seq", "wshard"),
                -distance,
            ).astype(jnp.float32),
            from_behind(
                grad_values_all[piece_start : piece_start + sent_rows].astype(jnp.bfloat16),
                ("seq", "wshard"),
                -distance,
            ).astype(jnp.float32),
        )
        back_keys = back_keys + arrived[0]
        back_values = back_values + arrived[1]
    own_keys = grad_keys_all[WINDOW:]
    own_values = grad_values_all[WINDOW:]
    split_row = row_count - sent_rows
    grad_keys = jnp.concatenate([own_keys[:split_row], own_keys + back_keys], 0)
    grad_values = jnp.concatenate([own_values[:split_row], own_values + back_values], 0).astype(
        jnp.bfloat16
    )

    def query_path(tensor, gain_vec):
        return norm_rope(tensor, gain_vec, cos_table, sin_table)

    _, pullback = jax.vjp(query_path, query_raw, query_gain)
    grad_query_raw, grad_gain_query = pullback(grad_queries)
    _, pullback = jax.vjp(query_path, key_raw, key_gain)
    grad_key_raw, grad_gain_key = pullback(grad_keys[:, None, :])
    grad_query_raw = grad_query_raw.reshape(row_count, head_count * head_dim).astype(jnp.bfloat16)
    grad_key_raw = grad_key_raw[:, 0].astype(jnp.bfloat16)
    grad_w_query = weight_grad(normed_in, grad_query_raw)
    grad_w_key = weight_grad(normed_in, grad_key_raw)
    grad_w_value = weight_grad(normed_in, grad_values)
    grad_normed_in = lax.dot_general(
        grad_query_raw, full_query, (((1,), (1,)), ((), ())), preferred_element_type=jnp.float32
    )
    grad_normed_in = grad_normed_in + lax.dot_general(
        grad_key_raw, full_key, (((1,), (1,)), ((), ())), preferred_element_type=jnp.float32
    )
    grad_normed_in = grad_normed_in + lax.dot_general(
        grad_values, full_value, (((1,), (1,)), ((), ())), preferred_element_type=jnp.float32
    )
    _, pullback = jax.vjp(rms_gain, x_float, in_gain)
    grad_input_part, grad_gain_in = pullback(grad_normed_in)
    grad_inputs = grad_resid + grad_input_part
    attn_gradients = (
        grad_w_query,
        grad_w_key,
        grad_w_value,
        grad_w_out,
        grad_gain_in,
        grad_gain_attn_post,
        grad_gain_query,
        grad_gain_key,
    )
    attn_parts = (
        lax.psum_scatter(
            attn_gradients[0].astype(jnp.bfloat16), "wshard", scatter_dimension=0, tiled=True
        ).astype(jnp.float32),
        lax.psum_scatter(
            attn_gradients[1].astype(jnp.bfloat16), "wshard", scatter_dimension=0, tiled=True
        ).astype(jnp.float32),
        lax.psum_scatter(
            attn_gradients[2].astype(jnp.bfloat16), "wshard", scatter_dimension=0, tiled=True
        ).astype(jnp.float32),
        lax.psum_scatter(
            attn_gradients[3].astype(jnp.bfloat16), "wshard", scatter_dimension=0, tiled=True
        ).astype(jnp.float32),
        lax.psum_scatter(
            attn_gradients[4].astype(jnp.bfloat16), "wshard", scatter_dimension=0, tiled=True
        ).astype(jnp.float32),
        lax.psum_scatter(
            attn_gradients[5].astype(jnp.bfloat16), "wshard", scatter_dimension=0, tiled=True
        ).astype(jnp.float32),
        lax.psum_scatter(
            attn_gradients[6].astype(jnp.bfloat16), "wshard", scatter_dimension=0, tiled=True
        ).astype(jnp.float32),
        lax.psum_scatter(
            attn_gradients[7].astype(jnp.bfloat16), "wshard", scatter_dimension=0, tiled=True
        ).astype(jnp.float32),
    )
    attn_reduced = (
        lax.psum(attn_parts[0].astype(jnp.bfloat16), "seq").astype(jnp.float32),
        lax.psum(attn_parts[1].astype(jnp.bfloat16), "seq").astype(jnp.float32),
        lax.psum(attn_parts[2].astype(jnp.bfloat16), "seq").astype(jnp.float32),
        lax.psum(attn_parts[3].astype(jnp.bfloat16), "seq").astype(jnp.float32),
        lax.psum(attn_parts[4].astype(jnp.bfloat16), "seq").astype(jnp.float32),
        lax.psum(attn_parts[5].astype(jnp.bfloat16), "seq").astype(jnp.float32),
        lax.psum(attn_parts[6].astype(jnp.bfloat16), "seq").astype(jnp.float32),
        lax.psum(attn_parts[7].astype(jnp.bfloat16), "seq").astype(jnp.float32),
    )
    reduced = (
        attn_reduced[0],
        attn_reduced[1],
        attn_reduced[2],
        attn_reduced[3],
        ff_reduced[0],
        ff_reduced[1],
        ff_reduced[2],
        attn_reduced[4],
        attn_reduced[5],
        ff_reduced[3],
        ff_reduced[4],
        attn_reduced[6],
        attn_reduced[7],
    )
    return (layer_out, grad_inputs) + tuple(reduced)


def solution(mesh):
    return jax.shard_map(
        per_device,
        mesh=mesh,
        in_specs=(
            P(("seq", "wshard"), None),
            P(("seq", "wshard")),
            P("wshard", None),
            P("wshard", None),
            P("wshard", None),
            P("wshard", None),
            P("wshard", None),
            P("wshard", None),
            P("wshard", None),
            P("wshard"),
            P("wshard"),
            P("wshard"),
            P("wshard"),
            P("wshard"),
            P("wshard"),
            P(("seq", "wshard"), None),
        ),
        out_specs=(
            P(("seq", "wshard"), None),
            P(("seq", "wshard"), None),
            P("wshard", None),
            P("wshard", None),
            P("wshard", None),
            P("wshard", None),
            P("wshard", None),
            P("wshard", None),
            P("wshard", None),
            P("wshard"),
            P("wshard"),
            P("wshard"),
            P("wshard"),
            P("wshard"),
            P("wshard"),
        ),
        check_vma=False,
    )
```

profile of v0, /device:TPU:0, one launch (start us, length us, event | category | flops | bytes accessed | tf_op | source)
XLA Modules:
  0.0 601.2 jit_solution(15135593721052747924)
XLA Ops:
  12.4 5.9 all-reduce.17
  18.3 9.8 %all_gather.40 = bf16[640,256]{1,0:T(8,128)(2,1)S(1)} all-gather(bf16[320,256]{1,0:T(8,128)(2,1)S(1)} %copy-done.40), channel_id=1, replica_groups=mesh['seq'=16,'wshard'=2] {'wshard'}, dimensions={0}, use_global_device_ids=true | all-gather | bytes 491520 | tf_op jit(solution)/shard_map/all_gather | solution.py:94
  29.1 4.4 collective-permute-start.1
  40.8 4.2 all-gather
  45.0 7.2 %all_gather.41 = bf16[640,256]{1,0:T(8,128)(2,1)S(1)} all-gather(bf16[320,256]{1,0:T(8,128)(2,1)S(1)} %copy-done.41), channel_id=1, replica_groups=mesh['seq'=16,'wshard'=2] {'wshard'}, dimensions={0}, use_global_device_ids=true | all-gather | bytes 491520 | tf_op jit(solution)/shard_map/all_gather | solution.py:93
  54.7 4.3 collective-permute-start.5
  59.7 5.4 all-gather.1
  78.5 33.6 %all-gather.12.cloned.1.call-done = bf16[640,2048]{1,0:T(8,128)(2,1)} async-done(((bf16[320,2048]{1,0:T(8,128)(2,1)}), bf16[640,2048]{1,0:T(8,128)(2,1)}) %all-gather.12.cloned.1.call-update) | async-done | bytes 2621456 | tf_op jit(solution)/shard_map/all_gather | solution.py:96
  112.1 4.0 fusion.93
  116.2 36.4 %all-gather.14.cloned.1.call-done = bf16[640,2048]{1,0:T(8,128)(2,1)} async-done(((bf16[320,2048]{1,0:T(8,128)(2,1)}), bf16[640,2048]{1,0:T(8,128)(2,1)}) %all-gather.14.cloned.1.call-update) | async-done | bytes 2621456 | tf_op jit(solution)/shard_map/all_gather | solution.py:97
  152.6 5.2 multiply_convert_fusion.1
  157.8 35.2 %all-gather.16.cloned.1.call-done = bf16[2048,640]{1,0:T(8,128)(2,1)} async-done(((bf16[1024,640]{1,0:T(8,128)(2,1)}), bf16[2048,640]{1,0:T(8,128)(2,1)}) %all-gather.16.cloned.1.call-update) | async-done | bytes 2621456 | tf_op jit(solution)/shard_map/all_gather | solution.py:98
  193.0 3.3 multiply_reduce_fusion.6
  211.4 8.0 %fusion.91 = (bf16[768,256]{0,1:T(8,128)(2,1)S(1)}, f32[768,256]{0,1:T(8,128)}) fusion(bf16[256,4,128]{2,0,1:T(8,128)(2,1)} %copy-done.39, bf16[256,4,128]{2,0,1:T(8,128)(2,1)S(1)} %copy-done.38, f32[768,256,4]{1,0,2:T(8,128)} %fusion.39, f32[4,256]{1,0:T(4,128)S(1)} %log_add_fusion, f32[768,256,4]{1,0,2:T(8,128)} %copy-done.7, ...), kind=kOutput, calls=%fused_computation.183 | convolution fusion | flops 414123776 | bytes 8196096 | tf_op jit(solution)/shard_map/hqk,qhd->kd/dot_general | solution.py:225
  222.8 8.2 %fusion.15 = f32[256,4,256]{2,0,1:T(8,128)} fusion(f32[768,256,4]{1,0,2:T(8,128)} %fusion.39, bf16[256,256]{0,1:T(8,128)(2,1)} %maximum_bitcast_fusion.6, bf16[256,256]{0,1:T(8,128)(2,1)} %collective-permute-done.5, bf16[256,256]{0,1:T(8,128)(2,1)} %collective-permute-done.4, f32[768,256,4]{1,0,2:T(8,128)} %copy-done.7, f32[4,256]{1,0:T(4,128)S(1)} %log_add_fusion, ...), kind=kOutput, calls=%fused_computation.31 | convolution fusion | flops 414058240 | bytes 7933952 | tf_op jit(solution)/shard_map/hqk,kd->qhd/dot_general | solution.py:222
  261.7 11.3 %reduce-scatter.12.cloned.1.call-done = bf16[320,256]{1,0:T(8,128)(2,1)} async-done(((bf16[640,256]{1,0:T(8,128)(2,1)}), bf16[320,256]{1,0:T(8,128)(2,1)}) %reduce-scatter.12.cloned.1.call-update) | async-done | bytes 163856 | tf_op jit(solution)/shard_map/reduce_scatter | solution.py:299
  273.1 26.1 %reduce-scatter.8.cloned.1.call-done = bf16[320,1024]{1,0:T(8,128)(2,1)} async-done(((bf16[640,1024]{1,0:T(8,128)(2,1)}), bf16[320,1024]{1,0:T(8,128)(2,1)}) %reduce-scatter.8.cloned.1.call-update) | async-done | bytes 655376 | tf_op jit(solution)/shard_map/reduce_scatter | solution.py:293
  299.2 26.1 %reduce-scatter.14.cloned.1.call-done = bf16[512,640]{1,0:T(8,128)(2,1)} async-done(((bf16[1024,640]{1,0:T(8,128)(2,1)}), bf16[512,640]{1,0:T(8,128)(2,1)}) %reduce-scatter.14.cloned.1.call-update) | async-done | bytes 655376 | tf_op jit(solution)/shard_map/reduce_scatter | solution.py:302
  325.3 40.4 %reduce-scatter.16.cloned.1.call-done = bf16[320,2048]{1,0:T(8,128)(2,1)} async-done(((bf16[640,2048]{1,0:T(8,128)(2,1)}), bf16[320,2048]{1,0:T(8,128)(2,1)}) %reduce-scatter.16.cloned.1.call-update) | async-done | bytes 1310736 | tf_op jit(solution)/shard_map/reduce_scatter | solution.py:184
  365.7 40.5 %reduce-scatter.18.cloned.1.call-done = bf16[320,2048]{1,0:T(8,128)(2,1)} async-done(((bf16[640,2048]{1,0:T(8,128)(2,1)}), bf16[320,2048]{1,0:T(8,128)(2,1)}) %reduce-scatter.18.cloned.1.call-update) | async-done | bytes 1310736 | tf_op jit(solution)/shard_map/reduce_scatter | solution.py:187
  406.2 40.4 %reduce-scatter.20.cloned.1.call-done = bf16[1024,640]{1,0:T(8,128)(2,1)} async-done(((bf16[2048,640]{1,0:T(8,128)(2,1)}), bf16[1024,640]{1,0:T(8,128)(2,1)}) %reduce-scatter.20.cloned.1.call-update) | async-done | bytes 1310736 | tf_op jit(solution)/shard_map/reduce_scatter | solution.py:190
  450.4 5.1 all-reduce.16
  455.9 34.5 %all-reduce.14 = (bf16[320]{0:T(512)(128)(2,1)S(1)}, bf16[320]{0:T(512)(128)(2,1)S(1)}, bf16[320]{0:T(512)(128)(2,1)S(1)}, bf16[320]{0:T(512)(128)(2,1)S(1)}, bf...) all-reduce(bf16[320]{0:T(512)(128)(2,1)S(1)} %dynamic-slice.5, ...), channel_id=1, replica_groups=mesh['seq'=16,'wshard'=2] {'seq'}, use_global_device_ids=true, to_apply=%region_31.32 | all-reduce | flops 1536 | bytes 6144 | tf_op jit(solution)/shard_map/psum | solution.py:323
  494.9 87.6 %all-reduce.20.cloned.1.call-done = (bf16[320,1024]{1,0:T(8,128)(2,1)}, bf16[320,256]{1,0:T(8,128)(2,1)}, bf16[320,256]{1,0:T(8,128)(2,1)}, bf16[512,640]{1,0:T(...) async-done(((bf16[320,1024]{1,0:T(8,128)(2,1)}, bf16[320,256]{1,0:T(8,128)(2,1)}, bf16[320,256]{1,0:T(8,128)(2,1)}, ...) | async-done | bytes 5570576 | tf_op jit(solution)/shard_map/psum | solution.py:319
  (268 shorter events, 97.0 us)
Async XLA Ops:
  7.3 60.6 %all-gather.8.cloned.1.call-start = ((), (), s32[]{:S(2)}) async-start(), calls=%async_computation.7 | async-start | bytes 1966080 | tf_op jit(solution)/shard_map/all_gather | solution.py:92
  8.0 67.9 %all-gather.10.cloned.1.call-start = ((), (), s32[]{:S(2)}) async-start(), calls=%async_computation.8 | async-start | bytes 1966080 | tf_op jit(solution)/shard_map/all_gather | solution.py:95
  8.8 103.4 %all-gather.12.cloned.1.call-start = ((), (), s32[]{:S(2)}) async-start(), calls=%async_computation.9 | async-start | bytes 3932160 | tf_op jit(solution)/shard_map/all_gather | solution.py:96
  9.5 143.0 %all-gather.14.cloned.1.call-start = ((), (), s32[]{:S(2)}) async-start(), calls=%async_computation.10 | async-start | bytes 3932160 | tf_op jit(solution)/shard_map/all_gather | solution.py:97
  10.1 182.9 %all-gather.16.cloned.1.call-start = ((), (), s32[]{:S(2)}) async-start(), calls=%async_computation.11 | async-start | bytes 3932160 | tf_op jit(solution)/shard_map/all_gather | solution.py:98
  29.1 44.8 %collective-permute-start.1 = (bf16[256,256]{1,0:T(8,128)(2,1)S(1)}, bf16[256,256]{1,0:T(8,128)(2,1)S(1)}, u32[]{:S(2)}, u32[]{:S(2)}) collective-permute-start(bf16[256,256]{1,0:T(8,128)(2,1)S(1)} %convolution_convert_fusion.9), channel_id=1, source_target_pairs={{0,1},{1,2},{2,3},{3,4},{4,5},{5,6},{6,7},{7,8},{8,9},{9,10},{10,1... | collective-permute-start | bytes 393224 | tf_op jit(solution)/shard_map/ppermute | solution.py:15
  33.5 40.4 %collective-permute-start = (bf16[256,256]{1,0:T(8,128)(2,1)S(1)}, bf16[256,256]{1,0:T(8,128)(2,1)S(1)}, u32[]{:S(2)}, u32[]{:S(2)}) collective-permute-start(bf16[256,256]{1,0:T(8,128)(2,1)S(1)} %convolution_convert_fusion.9), channel_id=1, source_target_pairs={{0,2},{1,3},{2,4},{3,5},{4,6},{5,7},{6,8},{7,9},{8,10},{9,11},{10,... | collective-permute-start | bytes 393224 | tf_op jit(solution)/shard_map/ppermute | solution.py:15
  34.9 30.2 %collective-permute-start.3 = (s32[256]{0:T(256)S(1)}, s32[256]{0:T(256)S(1)}, u32[]{:S(2)}, u32[]{:S(2)}) collective-permute-start(s32[256]{0:T(256)S(1)} %copy-done.48), channel_id=1, source_target_pairs={{0,1},{1,2},{2,3},{3,4},{4,5},{5,6},{6,7},{7,8},{8,9},{9,10},{10,1... | collective-permute-start | bytes 3080 | tf_op jit(solution)/shard_map/ppermute | solution.py:15
  38.0 29.0 %collective-permute-start.2 = (s32[256]{0:T(256)S(1)}, s32[256]{0:T(256)S(1)}, u32[]{:S(2)}, u32[]{:S(2)}) collective-permute-start(s32[256]{0:T(256)S(1)} %copy-done.48), channel_id=1, source_target_pairs={{0,2},{1,3},{2,4},{3,5},{4,6},{5,7},{6,8},{7,9},{8,10},{9,11},{10,... | collective-permute-start | bytes 3080 | tf_op jit(solution)/shard_map/ppermute | solution.py:15
  54.7 16.5 %collective-permute-start.5 = (bf16[256,256]{0,1:T(8,128)(2,1)}, bf16[256,256]{0,1:T(8,128)(2,1)}, u32[]{:S(2)}, u32[]{:S(2)}) collective-permute-start(bf16[256,256]{0,1:T(8,128)(2,1)} %maximum_bitcast_fusion.6), channel_id=1, source_target_pairs={{0,1},{1,2},{2,3},{3,4},{4,5},{5,6},{6,7},{7,8},{8,9},{9,10},{10,1... | collective-permute-start | bytes 393224 | tf_op jit(solution)/shard_map/ppermute | solution.py:15
  59.0 202.7 %reduce-scatter.10.cloned.1.call-start = ((), (), s32[]{:S(2)}) async-start(), calls=%async_computation.13 | async-start | bytes 491520 | tf_op jit(solution)/shard_map/reduce_scatter | solution.py:296
  65.1 6.1 %collective-permute-start.4 = (bf16[256,256]{0,1:T(8,128)(2,1)}, bf16[256,256]{0,1:T(8,128)(2,1)}, u32[]{:S(2)}, u32[]{:S(2)}) collective-permute-start(bf16[256,256]{0,1:T(8,128)(2,1)} %maximum_bitcast_fusion.6), channel_id=1, source_target_pairs={{0,2},{1,3},{2,4},{3,5},{4,6},{5,7},{6,8},{7,9},{8,10},{9,11},{10,... | collective-permute-start | bytes 393224 | tf_op jit(solution)/shard_map/ppermute | solution.py:15
  220.1 16.6 %collective-permute-start.7 = (bf16[256,256]{0,1:T(8,128)(2,1)}, bf16[256,256]{0,1:T(8,128)(2,1)}, u32[]{:S(2)}, u32[]{:S(2)}) collective-permute-start(bf16[256,256]{0,1:T(8,128)(2,1)} %get-tuple-element.64), channel_id=1, source_target_pairs={{1,0},{2,1},{3,2},{4,3},{5,4},{6,5},{7,6},{8,7},{9,8},{10,9},{11,1... | collective-permute-start | bytes 393224 | tf_op jit(solution)/shard_map/ppermute | solution.py:15
  221.4 15.3 %collective-permute-start.6 = (bf16[256,256]{0,1:T(8,128)(2,1)}, bf16[256,256]{0,1:T(8,128)(2,1)}, u32[]{:S(2)}, u32[]{:S(2)}) collective-permute-start(bf16[256,256]{0,1:T(8,128)(2,1)} %get-tuple-element.63), channel_id=1, source_target_pairs={{2,0},{3,1},{4,2},{5,3},{6,4},{7,5},{8,6},{9,7},{10,8},{11,9},{12,... | collective-permute-start | bytes 393224 | tf_op jit(solution)/shard_map/ppermute | solution.py:15
  234.1 8.7 %collective-permute-start.9 = (bf16[256,256]{1,0:T(8,128)(2,1)}, bf16[256,256]{1,0:T(8,128)(2,1)S(1)}, u32[]{:S(2)}, u32[]{:S(2)}) collective-permute-start(bf16[256,256]{1,0:T(8,128)(2,1)} %get-tuple-element.62), channel_id=1, source_target_pairs={{1,0},{2,1},{3,2},{4,3},{5,4},{6,5},{7,6},{8,7},{9,8},{10,9},{11,1... | collective-permute-start | bytes 393224 | tf_op jit(solution)/shard_map/ppermute | solution.py:15
  235.4 7.4 %collective-permute-start.8 = (bf16[256,256]{1,0:T(8,128)(2,1)S(1)}, bf16[256,256]{1,0:T(8,128)(2,1)S(1)}, u32[]{:S(2)}, u32[]{:S(2)}) collective-permute-start(bf16[256,256]{1,0:T(8,128)(2,1)S(1)} %get-tuple-element.61), channel_id=1, source_target_pairs={{2,0},{3,1},{4,2},{5,3},{6,4},{7,5},{8,6},{9,7},{10,8},{11,9},{12,... | collective-permute-start | bytes 393224 | tf_op jit(solution)/shard_map/ppermute | solution.py:15
  240.5 32.6 %reduce-scatter.12.cloned.1.call-start = ((), (), s32[]{:S(2)}) async-start(), calls=%async_computation.14 | async-start | bytes 491520 | tf_op jit(solution)/shard_map/reduce_scatter | solution.py:299
  245.5 53.6 %reduce-scatter.8.cloned.1.call-start = ((), (), s32[]{:S(2)}) async-start(), calls=%async_computation.12 | async-start | bytes 1966080 | tf_op jit(solution)/shard_map/reduce_scatter | solution.py:293
  250.1 75.3 %reduce-scatter.14.cloned.1.call-start = ((), (), s32[]{:S(2)}) async-start(), calls=%async_computation.15 | async-start | bytes 1966080 | tf_op jit(solution)/shard_map/reduce_scatter | solution.py:302
  251.8 113.9 %reduce-scatter.16.cloned.1.call-start = ((), (), s32[]{:S(2)}) async-start(), calls=%async_computation.16 | async-start | bytes 3932160 | tf_op jit(solution)/shard_map/reduce_scatter | solution.py:184
  254.2 152.0 %reduce-scatter.18.cloned.1.call-start = ((), (), s32[]{:S(2)}) async-start(), calls=%async_computation.17 | async-start | bytes 3932160 | tf_op jit(solution)/shard_map/reduce_scatter | solution.py:187
  257.8 188.8 %reduce-scatter.20.cloned.1.call-start = ((), (), s32[]{:S(2)}) async-start(), calls=%async_computation.18 | async-start | bytes 3932160 | tf_op jit(solution)/shard_map/reduce_scatter | solution.py:190
  261.7 320.8 %all-reduce.20.cloned.1.call-start = ((), (), s32[]{:S(2)}) async-start(), calls=%async_computation.19 | async-start | bytes 11141120 | tf_op jit(solution)/shard_map/psum | solution.py:319
  448.4 45.4 %copy-start.2 = (f32[256,640]{1,0:T(8,128)S(1)}, f32[256,640]{1,0:T(8,128)}, u32[]{:S(2)}) copy-start(f32[256,640]{1,0:T(8,128)} %copy-done.1) | copy-start | bytes 1966084
  (57 other events, 387.8 us)
Sparse Core Ops, SparseCore 0:
  9.6 30.6 all-gather.7
  41.9 28.2 all-gather.9
  71.7 40.3 all-gather.11
  113.5 38.9 all-gather.13
  153.9 38.9 all-gather.15
  240.6 17.6 reduce-scatter.9
  260.5 12.4 reduce-scatter.11
  275.9 23.2 reduce-scatter.7
  302.0 23.2 reduce-scatter.13
  328.0 37.6 reduce-scatter.15
  368.5 37.6 reduce-scatter.17
  408.9 37.6 reduce-scatter.19
  451.3 131.1 all-reduce.19
where the time goes:
time: 602 us; the launch traced here: 601 us
  waiting for transfers between devices  382 us (63%)
  blocking collectives  72.1 us (12%)
  matrix products  61.4 us (10%)
  other arithmetic  29.2 us (5%)
  starting transfers between devices  23.9 us (4%)
  between operations  17 us (3%)
  local copies, waits for them, and re-layouts  15.4 us (3%)
    psum x1, waiting for transfers between devices, per_device(): lax.psum(attn_parts[0].astype(jnp.bfloat16), 'seq').astype(jnp.float32)  87.6 us
    reduce_scatter x1, waiting for transfers between devices, per_device(): lax.psum_scatter(ff_gradients[1].astype(jnp.bfloat16), 'wshard', scatter_...  40.5 us
    reduce_scatter x1, waiting for transfers between devices, per_device(): lax.psum_scatter(ff_gradients[2].astype(jnp.bfloat16), 'wshard', scatter_...  40.4 us
    reduce_scatter x1, waiting for transfers between devices, per_device(): lax.psum_scatter(ff_gradients[0].astype(jnp.bfloat16), 'wshard', scatter_...  40.4 us
    all_gather x1, waiting for transfers between devices, per_device(): lax.all_gather(w_up, 'wshard', axis=0, tiled=True)  36.4 us
    all_gather x1, waiting for transfers between devices, per_device(): lax.all_gather(w_down, 'wshard', axis=0, tiled=True)  35.2 us
    psum x1, blocking collectives, per_device(): lax.psum(attn_parts[4].astype(jnp.bfloat16), 'seq').astype(jnp.float32)  34.5 us
    all_gather x1, waiting for transfers between devices, per_device(): lax.all_gather(w_gate, 'wshard', axis=0, tiled=True)  33.6 us
  transfers between devices with their start and end apart: 23, of which 11 were waited for; matrix products, arithmetic and copies ran while one was open for 10% of the time, Pallas kernels for 0%

commit v1 on v0

--- a/solution.py
+++ b/solution.py
@@ -7,6 +7,27 @@
 NORM_EPSILON = 1e-06
 ROPE_BASE = 10000.0
 MASK_FLOOR = -1e30
+
+
+def in_order(tiles, dim):
+    shape = list(tiles.shape[1:])
+    shape[dim] *= tiles.shape[0]
+    return jnp.moveaxis(tiles, 0, dim).reshape(shape)
+
+
+def grow_blocks(shard, axis):
+    count, position = (lax.axis_size(axis), lax.axis_index(axis))
+    pieces, distance = (shard[None], 1)
+    while distance < count:
+        other = lax.ppermute(pieces, axis, [(i, i ^ distance) for i in range(count)])
+        low = position & distance == 0
+        pieces = jnp.concatenate([jnp.where(low, pieces, other), jnp.where(low, other, pieces)])
+        distance *= 2
+    return pieces
+
+
+def collect(x, axis, dim):
+    return in_order(grow_blocks(x, axis), dim)
 
 
 def from_behind(array, axis, by):
@@ -93,7 +114,7 @@
         lax.all_gather(w_key, "wshard", axis=0, tiled=True),
         lax.all_gather(w_value, "wshard", axis=0, tiled=True),
         lax.all_gather(w_out, "wshard", axis=0, tiled=True),
-        lax.all_gather(w_gate, "wshard", axis=0, tiled=True),
+        collect(w_gate, "wshard", 0),
         lax.all_gather(w_up, "wshard", axis=0, tiled=True),
         lax.all_gather(w_down, "wshard", axis=0, tiled=True),
         lax.all_gather(gain_in, "wshard", axis=0, tiled=True),

time: 602 us -> 578 us (0.960)
  waiting for transfers between devices: 382 us -> 354 us
    all_gather x1 -> x0, waiting for transfers between devices: 33.6 us -> none  [per_device(): lax.all_gather(w_gate, 'wshard', axis=0, tiled=True)]
    ppermute x0 -> x1, waiting for transfers between devices: none -> 22.2 us  [grow_blocks(): lax.ppermute(pieces, axis, [(i, i ^ distance) for i in range(count)])]
    all_gather x1, waiting for transfers between devices: 36.4 us -> 18.6 us  [per_device(): lax.all_gather(w_up, 'wshard', axis=0, tiled=True)]
    unnamed x131 -> x133, local copies, waits for them, and re-layouts: 11.2 us -> 12.7 us
  transfers between devices with their start and end apart: 23 -> 23, of which waited for: 11 -> 11; matrix products, arithmetic and copies ran while one was open for 10% -> 11% of each run, Pallas kernels for 0% -> 0%
where the time goes in v1:
time: 578 us; the launch traced here: 577 us
  waiting for transfers between devices  354 us (61%)
  blocking collectives  71.5 us (12%)
  matrix products  59.7 us (10%)
  other arithmetic  31.2 us (5%)
  starting transfers between devices  26.2 us (5%)
  between operations  17.3 us (3%)
  local copies, waits for them, and re-layouts  16.9 us (3%)
    psum x1, waiting for transfers between devices, per_device(): lax.psum(attn_parts[0].astype(jnp.bfloat16), 'seq').astype(jnp.float32)  87.6 us
    reduce_scatter x1, waiting for transfers between devices, per_device(): lax.psum_scatter(ff_gradients[0].astype(jnp.bfloat16), 'wshard', scatter_...  40.5 us
    reduce_scatter x1, waiting for transfers between devices, per_device(): lax.psum_scatter(ff_gradients[2].astype(jnp.bfloat16), 'wshard', scatter_...  40.5 us
    reduce_scatter x1, waiting for transfers between devices, per_device(): lax.psum_scatter(ff_gradients[1].astype(jnp.bfloat16), 'wshard', scatter_...  40.4 us
    all_gather x1, waiting for transfers between devices, per_device(): lax.all_gather(w_down, 'wshard', axis=0, tiled=True)  36.5 us
    psum x1, blocking collectives, per_device(): lax.psum(attn_parts[4].astype(jnp.bfloat16), 'seq').astype(jnp.float32)  34.4 us
    reduce_scatter x1, waiting for transfers between devices, per_device(): lax.psum_scatter(attn_gradients[0].astype(jnp.bfloat16), 'wshard', scatte...  26.1 us
    reduce_scatter x1, waiting for transfers between devices, per_device(): lax.psum_scatter(attn_gradients[3].astype(jnp.bfloat16), 'wshard', scatte...  26.1 us
  transfers between devices with their start and end apart: 23, of which 11 were waited for; matrix products, arithmetic and copies ran while one was open for 11% of the time, Pallas kernels for 0%

profile of v1, /device:TPU:0, one launch (start us, length us, event | category | flops | bytes accessed | tf_op | source)
XLA Modules:
  0.0 576.7 jit_solution(17956173886367294233)
XLA Ops:
  11.8 5.9 %all-reduce.17 = (bf16[640]{0:T(1024)(128)(2,1)S(1)}, bf16[640]{0:T(1024)(128)(2,1)S(1)}, bf16[640]{0:T(1024)(128)(2,1)S(1)}, bf16[640]{0:T(1024)(128)(2,1)S(1)}) all-reduce(bf16[640]{0:T(1024)(128)(2,1)S(1)} %dynamic-update-slice, bf16[640]{0:T(1024)(128)(2,1)S(1)} %dynamic-update-slice.1, ...), channel_id=1, replica_groups=mesh['seq'=16,'wshard'=2] {'wshard'}, use_global_device_ids=true, to_apply=%add.4 | all-reduce | flops 2560 | bytes 10240
  17.7 9.4 %all_gather.37 = bf16[640,256]{1,0:T(8,128)(2,1)S(1)} all-gather(bf16[320,256]{1,0:T(8,128)(2,1)S(1)} %copy-done.40), channel_id=1, replica_groups=mesh['seq'=16,'wshard'=2] {'wshard'}, dimensions={0}, use_global_device_ids=true | all-gather | bytes 491520 | tf_op jit(solution)/shard_map/all_gather | solution.py:115
  28.2 4.4 collective-permute-start.1
  33.9 3.5 collective-permute-start.3
  39.7 4.2 all-gather
  43.9 7.2 %all_gather.38 = bf16[640,256]{1,0:T(8,128)(2,1)S(1)} all-gather(bf16[320,256]{1,0:T(8,128)(2,1)S(1)} %copy-done.41), channel_id=1, replica_groups=mesh['seq'=16,'wshard'=2] {'wshard'}, dimensions={0}, use_global_device_ids=true | all-gather | bytes 491520 | tf_op jit(solution)/shard_map/all_gather | solution.py:114
  53.7 4.3 collective-permute-start.5
  58.6 5.4 all-gather.1
  79.9 22.2 %collective-permute-done.6 = bf16[1,320,2048]{2,1,0:T(8,128)(2,1)} collective-permute-done((bf16[1,320,2048]{2,1,0:T(8,128)(2,1)}, bf16[1,320,2048]{2,1,0:T(8,128)(2,1)}, u32[]{:S(2)}, u32[]{:S(2)}) %collective-permute-start.6) | collective-permute-done | bytes 1310752 | tf_op jit(solution)/shard_map/ppermute | solution.py:22
  108.1 18.6 %all-gather.11.cloned.1.call-done = bf16[640,2048]{1,0:T(8,128)(2,1)} async-done(((bf16[320,2048]{1,0:T(8,128)(2,1)}), bf16[640,2048]{1,0:T(8,128)(2,1)}) %all-gather.11.cloned.1.call-update) | async-done | bytes 2621456 | tf_op jit(solution)/shard_map/all_gather | solution.py:118
  126.6 5.2 multiply_convert_fusion.1
  131.9 36.5 %all-gather.13.cloned.1.call-done = bf16[2048,640]{1,0:T(8,128)(2,1)} async-done(((bf16[1024,640]{1,0:T(8,128)(2,1)}), bf16[2048,640]{1,0:T(8,128)(2,1)}) %all-gather.13.cloned.1.call-update) | async-done | bytes 2621456 | tf_op jit(solution)/shard_map/all_gather | solution.py:119
  168.4 3.3 multiply_reduce_fusion.6
  186.8 8.0 %fusion.91 = (bf16[768,256]{0,1:T(8,128)(2,1)S(1)}, f32[768,256]{0,1:T(8,128)}) fusion(bf16[256,4,128]{2,0,1:T(8,128)(2,1)} %copy-done.39, bf16[256,4,128]{2,0,1:T(8,128)(2,1)S(1)} %copy-done.38, f32[768,256,4]{1,0,2:T(8,128)} %fusion.39, f32[4,256]{1,0:T(4,128)S(1)} %log_add_fusion, f32[768,256,4]{1,0,2:T(8,128)} %copy-done.9, ...), kind=kOutput, calls=%fused_computation.186 | convolution fusion | flops 414123776 | bytes 8196096 | tf_op jit(solution)/shard_map/hqk,qhd->kd/dot_general | solution.py:246
  198.2 8.2 %fusion.15 = f32[256,4,256]{2,0,1:T(8,128)} fusion(f32[768,256,4]{1,0,2:T(8,128)} %fusion.39, bf16[256,256]{0,1:T(8,128)(2,1)} %maximum_bitcast_fusion.6, bf16[256,256]{0,1:T(8,128)(2,1)} %collective-permute-done.5, bf16[256,256]{0,1:T(8,128)(2,1)} %collective-permute-done.4, f32[768,256,4]{1,0,2:T(8,128)} %copy-done.9, f32[4,256]{1,0:T(4,128)S(1)} %log_add_fusion, ...), kind=kOutput, calls=%fused_computation.32 | convolution fusion | flops 414058240 | bytes 7933952 | tf_op jit(solution)/shard_map/hqk,kd->qhd/dot_general | solution.py:243
  237.1 11.2 %reduce-scatter.12.cloned.1.call-done = bf16[320,256]{1,0:T(8,128)(2,1)} async-done(((bf16[640,256]{1,0:T(8,128)(2,1)}), bf16[320,256]{1,0:T(8,128)(2,1)}) %reduce-scatter.12.cloned.1.call-update) | async-done | bytes 163856 | tf_op jit(solution)/shard_map/reduce_scatter | solution.py:320
  248.3 26.1 %reduce-scatter.8.cloned.1.call-done = bf16[320,1024]{1,0:T(8,128)(2,1)} async-done(((bf16[640,1024]{1,0:T(8,128)(2,1)}), bf16[320,1024]{1,0:T(8,128)(2,1)}) %reduce-scatter.8.cloned.1.call-update) | async-done | bytes 655376 | tf_op jit(solution)/shard_map/reduce_scatter | solution.py:314
  274.5 26.1 %reduce-scatter.14.cloned.1.call-done = bf16[512,640]{1,0:T(8,128)(2,1)} async-done(((bf16[1024,640]{1,0:T(8,128)(2,1)}), bf16[512,640]{1,0:T(8,128)(2,1)}) %reduce-scatter.14.cloned.1.call-update) | async-done | bytes 655376 | tf_op jit(solution)/shard_map/reduce_scatter | solution.py:323
  300.6 40.5 %reduce-scatter.16.cloned.1.call-done = bf16[320,2048]{1,0:T(8,128)(2,1)} async-done(((bf16[640,2048]{1,0:T(8,128)(2,1)}), bf16[320,2048]{1,0:T(8,128)(2,1)}) %reduce-scatter.16.cloned.1.call-update) | async-done | bytes 1310736 | tf_op jit(solution)/shard_map/reduce_scatter | solution.py:205
  341.1 40.4 %reduce-scatter.18.cloned.1.call-done = bf16[320,2048]{1,0:T(8,128)(2,1)} async-done(((bf16[640,2048]{1,0:T(8,128)(2,1)}), bf16[320,2048]{1,0:T(8,128)(2,1)}) %reduce-scatter.18.cloned.1.call-update) | async-done | bytes 1310736 | tf_op jit(solution)/shard_map/reduce_scatter | solution.py:208
  381.5 40.5 %reduce-scatter.20.cloned.1.call-done = bf16[1024,640]{1,0:T(8,128)(2,1)} async-done(((bf16[2048,640]{1,0:T(8,128)(2,1)}), bf16[1024,640]{1,0:T(8,128)(2,1)}) %reduce-scatter.20.cloned.1.call-update) | async-done | bytes 1310736 | tf_op jit(solution)/shard_map/reduce_scatter | solution.py:211
  425.8 5.1 all-reduce.16
  431.3 34.4 %all-reduce.14 = (bf16[320]{0:T(512)(128)(2,1)S(1)}, bf16[320]{0:T(512)(128)(2,1)S(1)}, bf16[320]{0:T(512)(128)(2,1)S(1)}, bf16[320]{0:T(512)(128)(2,1)S(1)}, bf...) all-reduce(bf16[320]{0:T(512)(128)(2,1)S(1)} %dynamic-slice.5, ...), channel_id=1, replica_groups=mesh['seq'=16,'wshard'=2] {'seq'}, use_global_device_ids=true, to_apply=%region_31.32 | all-reduce | flops 1536 | bytes 6144 | tf_op jit(solution)/shard_map/psum | solution.py:344
  470.1 87.6 %all-reduce.20.cloned.1.call-done = (bf16[320,1024]{1,0:T(8,128)(2,1)}, bf16[320,256]{1,0:T(8,128)(2,1)}, bf16[320,256]{1,0:T(8,128)(2,1)}, bf16[512,640]{1,0:T(...) async-done(((bf16[320,1024]{1,0:T(8,128)(2,1)}, bf16[320,256]{1,0:T(8,128)(2,1)}, bf16[320,256]{1,0:T(8,128)(2,1)}, ...) | async-done | bytes 5570576 | tf_op jit(solution)/shard_map/psum | solution.py:340
  (271 shorter events, 101.3 us)
Async XLA Ops:
  7.3 61.9 %all-gather.7.cloned.1.call-start = ((), (), s32[]{:S(2)}) async-start(), calls=%async_computation.7 | async-start | bytes 1966080 | tf_op jit(solution)/shard_map/all_gather | solution.py:113
  8.0 69.3 %all-gather.9.cloned.1.call-start = ((), (), s32[]{:S(2)}) async-start(), calls=%async_computation.8 | async-start | bytes 1966080 | tf_op jit(solution)/shard_map/all_gather | solution.py:116
  8.8 117.9 %all-gather.11.cloned.1.call-start = ((), (), s32[]{:S(2)}) async-start(), calls=%async_computation.9 | async-start | bytes 3932160 | tf_op jit(solution)/shard_map/all_gather | solution.py:118
  9.5 158.9 %all-gather.13.cloned.1.call-start = ((), (), s32[]{:S(2)}) async-start(), calls=%async_computation.10 | async-start | bytes 3932160 | tf_op jit(solution)/shard_map/all_gather | solution.py:119
  28.2 47.3 %copy-start.42 = (bf16[256,256]{1,0:T(8,128)(2,1)}, bf16[256,256]{1,0:T(8,128)(2,1)S(1)}, u32[]{:S(2)}) copy-start(bf16[256,256]{1,0:T(8,128)(2,1)S(1)} %convolution_convert_fusion.9) | copy-start | bytes 393220
  28.2 47.2 %collective-permute-start.1 = (bf16[256,256]{1,0:T(8,128)(2,1)S(1)}, bf16[256,256]{1,0:T(8,128)(2,1)S(1)}, u32[]{:S(2)}, u32[]{:S(2)}) collective-permute-start(bf16[256,256]{1,0:T(8,128)(2,1)S(1)} %convolution_convert_fusion.9), channel_id=1, source_target_pairs={{0,1},{1,2},{2,3},{3,4},{4,5},{5,6},{6,7},{7,8},{8,9},{9,10},{10,1... | collective-permute-start | bytes 393224 | tf_op jit(solution)/shard_map/ppermute | solution.py:36
  32.6 42.8 %collective-permute-start = (bf16[256,256]{1,0:T(8,128)(2,1)S(1)}, bf16[256,256]{1,0:T(8,128)(2,1)S(1)}, u32[]{:S(2)}, u32[]{:S(2)}) collective-permute-start(bf16[256,256]{1,0:T(8,128)(2,1)S(1)} %convolution_convert_fusion.9), channel_id=1, source_target_pairs={{0,2},{1,3},{2,4},{3,5},{4,6},{5,7},{6,8},{7,9},{8,10},{9,11},{10,... | collective-permute-start | bytes 393224 | tf_op jit(solution)/shard_map/ppermute | solution.py:36
  33.9 30.1 %collective-permute-start.3 = (s32[256]{0:T(256)S(1)}, s32[256]{0:T(256)S(1)}, u32[]{:S(2)}, u32[]{:S(2)}) collective-permute-start(s32[256]{0:T(256)S(1)} %copy-done.48), channel_id=1, source_target_pairs={{0,1},{1,2},{2,3},{3,4},{4,5},{5,6},{6,7},{7,8},{8,9},{9,10},{10,1... | collective-permute-start | bytes 3080 | tf_op jit(solution)/shard_map/ppermute | solution.py:36
  37.4 28.6 %collective-permute-start.2 = (s32[256]{0:T(256)S(1)}, s32[256]{0:T(256)S(1)}, u32[]{:S(2)}, u32[]{:S(2)}) collective-permute-start(s32[256]{0:T(256)S(1)} %copy-done.48), channel_id=1, source_target_pairs={{0,2},{1,3},{2,4},{3,5},{4,6},{5,7},{6,8},{7,9},{8,10},{9,11},{10,... | collective-permute-start | bytes 3080 | tf_op jit(solution)/shard_map/ppermute | solution.py:36
  53.7 18.9 %collective-permute-start.5 = (bf16[256,256]{0,1:T(8,128)(2,1)}, bf16[256,256]{0,1:T(8,128)(2,1)}, u32[]{:S(2)}, u32[]{:S(2)}) collective-permute-start(bf16[256,256]{0,1:T(8,128)(2,1)} %maximum_bitcast_fusion.6), channel_id=1, source_target_pairs={{0,1},{1,2},{2,3},{3,4},{4,5},{5,6},{6,7},{7,8},{8,9},{9,10},{10,1... | collective-permute-start | bytes 393224 | tf_op jit(solution)/shard_map/ppermute | solution.py:36
  58.0 179.2 %reduce-scatter.10.cloned.1.call-start = ((), (), s32[]{:S(2)}) async-start(), calls=%async_computation.12 | async-start | bytes 491520 | tf_op jit(solution)/shard_map/reduce_scatter | solution.py:317
  64.0 8.6 %collective-permute-start.4 = (bf16[256,256]{0,1:T(8,128)(2,1)}, bf16[256,256]{0,1:T(8,128)(2,1)}, u32[]{:S(2)}, u32[]{:S(2)}) collective-permute-start(bf16[256,256]{0,1:T(8,128)(2,1)} %maximum_bitcast_fusion.6), channel_id=1, source_target_pairs={{0,2},{1,3},{2,4},{3,5},{4,6},{5,7},{6,8},{7,9},{8,10},{9,11},{10,... | collective-permute-start | bytes 393224 | tf_op jit(solution)/shard_map/ppermute | solution.py:36
  66.0 36.1 %collective-permute-start.6 = (bf16[1,320,2048]{2,1,0:T(8,128)(2,1)}, bf16[1,320,2048]{2,1,0:T(8,128)(2,1)}, u32[]{:S(2)}, u32[]{:S(2)}) collective-permute-start(bf16[1,320,2048]{2,1,0:T(8,128)(2,1)} %bitcast.12), channel_id=1, source_target_pairs={{0,1},{1,0},{2,3},{3,2},{4,5},{5,4},{6,7},{7,6},{8,9},{9,8},{10,11... | collective-permute-start | bytes 3932168 | tf_op jit(solution)/shard_map/ppermute | solution.py:22
  195.5 16.6 %collective-permute-start.8 = (bf16[256,256]{0,1:T(8,128)(2,1)}, bf16[256,256]{0,1:T(8,128)(2,1)}, u32[]{:S(2)}, u32[]{:S(2)}) collective-permute-start(bf16[256,256]{0,1:T(8,128)(2,1)} %get-tuple-element.66), channel_id=1, source_target_pairs={{1,0},{2,1},{3,2},{4,3},{5,4},{6,5},{7,6},{8,7},{9,8},{10,9},{11,1... | collective-permute-start | bytes 393224 | tf_op jit(solution)/shard_map/ppermute | solution.py:36
  196.8 15.3 %collective-permute-start.7 = (bf16[256,256]{0,1:T(8,128)(2,1)}, bf16[256,256]{0,1:T(8,128)(2,1)}, u32[]{:S(2)}, u32[]{:S(2)}) collective-permute-start(bf16[256,256]{0,1:T(8,128)(2,1)} %get-tuple-element.65), channel_id=1, source_target_pairs={{2,0},{3,1},{4,2},{5,3},{6,4},{7,5},{8,6},{9,7},{10,8},{11,9},{12,... | collective-permute-start | bytes 393224 | tf_op jit(solution)/shard_map/ppermute | solution.py:36
  209.5 8.7 %collective-permute-start.10 = (bf16[256,256]{1,0:T(8,128)(2,1)}, bf16[256,256]{1,0:T(8,128)(2,1)S(1)}, u32[]{:S(2)}, u32[]{:S(2)}) collective-permute-start(bf16[256,256]{1,0:T(8,128)(2,1)} %get-tuple-element.64), channel_id=1, source_target_pairs={{1,0},{2,1},{3,2},{4,3},{5,4},{6,5},{7,6},{8,7},{9,8},{10,9},{11,1... | collective-permute-start | bytes 393224 | tf_op jit(solution)/shard_map/ppermute | solution.py:36
  210.8 7.4 %collective-permute-start.9 = (bf16[256,256]{1,0:T(8,128)(2,1)S(1)}, bf16[256,256]{1,0:T(8,128)(2,1)S(1)}, u32[]{:S(2)}, u32[]{:S(2)}) collective-permute-start(bf16[256,256]{1,0:T(8,128)(2,1)S(1)} %get-tuple-element.63), channel_id=1, source_target_pairs={{2,0},{3,1},{4,2},{5,3},{6,4},{7,5},{8,6},{9,7},{10,8},{11,9},{12,... | collective-permute-start | bytes 393224 | tf_op jit(solution)/shard_map/ppermute | solution.py:36
  215.9 32.4 %reduce-scatter.12.cloned.1.call-start = ((), (), s32[]{:S(2)}) async-start(), calls=%async_computation.13 | async-start | bytes 491520 | tf_op jit(solution)/shard_map/reduce_scatter | solution.py:320
  220.9 53.5 %reduce-scatter.8.cloned.1.call-start = ((), (), s32[]{:S(2)}) async-start(), calls=%async_computation.11 | async-start | bytes 1966080 | tf_op jit(solution)/shard_map/reduce_scatter | solution.py:314
  225.5 75.1 %reduce-scatter.14.cloned.1.call-start = ((), (), s32[]{:S(2)}) async-start(), calls=%async_computation.14 | async-start | bytes 1966080 | tf_op jit(solution)/shard_map/reduce_scatter | solution.py:323
  227.2 113.9 %reduce-scatter.16.cloned.1.call-start = ((), (), s32[]{:S(2)}) async-start(), calls=%async_computation.15 | async-start | bytes 3932160 | tf_op jit(solution)/shard_map/reduce_scatter | solution.py:205
  229.6 151.9 %reduce-scatter.18.cloned.1.call-start = ((), (), s32[]{:S(2)}) async-start(), calls=%async_computation.16 | async-start | bytes 3932160 | tf_op jit(solution)/shard_map/reduce_scatter | solution.py:208
  233.2 188.8 %reduce-scatter.20.cloned.1.call-start = ((), (), s32[]{:S(2)}) async-start(), calls=%async_computation.17 | async-start | bytes 3932160 | tf_op jit(solution)/shard_map/reduce_scatter | solution.py:211
  237.1 320.6 %all-reduce.20.cloned.1.call-start = ((), (), s32[]{:S(2)}) async-start(), calls=%async_computation.18 | async-start | bytes 11141120 | tf_op jit(solution)/shard_map/psum | solution.py:340
  (58 other events, 388.0 us)
Sparse Core Ops, SparseCore 0:
  9.6 30.0 all-gather.6
  41.3 29.0 all-gather.8
  71.9 54.6 all-gather.10
  128.0 40.2 all-gather.12
  216.0 17.6 reduce-scatter.9
  235.8 12.4 reduce-scatter.11
  251.2 23.2 reduce-scatter.7
  277.3 23.2 reduce-scatter.13
  303.4 37.6 reduce-scatter.15
  343.8 37.6 reduce-scatter.17
  384.3 37.6 reduce-scatter.19
  426.6 131.0 all-reduce.19
